TPU v7x, 32 devices: a whole 2x2x4 slice. The times are simulated.
32 devices in a mesh: rows: 8 (over y, x, core), chan: 4 (over z).
Axes of the slice: x: 2, y: 2, z: 4, core: 2. Of those that a mesh axis runs over, the one named last changes fastest.
Arguments:
- latents: bfloat16 [512, 4, 8, 128], P('chan', None, 'rows'), may hold values from -20 to 20
- cache_one: bfloat16 [512, 2, 8, 128], P('chan', None, 'rows'), may hold values from -4 to 4
- cache_two: bfloat16 [512, 2, 8, 128], P('chan', None, 'rows'), may hold values from -4 to 4
- gain_one: float32 [512], P('chan'), may hold values from 0.25 to 1.75
- bias_one: float32 [512], P('chan'), may hold values from -0.8 to 0.8
- weight_one: bfloat16 [3, 3, 3, 512, 512], P(None, None, None, None, 'chan'), may hold values from -0.0546875 to 0.0546875
- gain_two: float32 [512], P('chan'), may hold values from 0.25 to 1.75
- bias_two: float32 [512], P('chan'), may hold values from -0.8 to 0.8
- weight_two: bfloat16 [3, 3, 3, 512, 512], P(None, None, None, 'chan'), may hold values from -0.0625 to 0.0625
Outputs:
- upsampled: float32 [512, 4, 16, 256], P('chan', None, 'rows')
All inputs are finite; a program needn't handle non-finite values.
Results may differ from a plain program's by a relative error of at most 0.0022.
Values may be sent and summed in bfloat16 or wider, within the bound.
A program may use at most 64 MiB of HBM per device.

v0:
```python
import jax
import jax.numpy as jnp
from jax import lax
from jax.sharding import PartitionSpec as P

CHANNELS = 512
GROUPS = 32
epsilon = 1e-06


def padded(block, sides, width):
    for axis, dim in sides:
        count = lax.axis_size(axis)
        forward = [(i, i + 1) for i in range(count - 1)]
        backward = [(target, source) for source, target in forward]
        low = lax.ppermute(
            lax.slice_in_dim(block, block.shape[dim] - width, None, axis=dim), axis, forward
        )
        high = lax.ppermute(lax.slice_in_dim(block, 0, width, axis=dim), axis, backward)
        block = jnp.concatenate([low, block, high], axis=dim)
    return block


def group_silu(values, gain, bias):
    group_size = CHANNELS // GROUPS
    grouped = values.reshape(values.shape[0] // group_size, -1)
    sums, squares = lax.psum((jnp.sum(grouped, axis=1), jnp.sum(grouped * grouped, axis=1)), "rows")
    members = grouped.shape[1] * lax.axis_size("rows")
    average = sums / members
    spread = squares / members - average * average
    normed = ((grouped - average[:, None]) * lax.rsqrt(spread + epsilon)[:, None]).reshape(
        values.shape
    )
    scaled = normed * gain[:, None, None, None] + bias[:, None, None, None]
    return jax.nn.silu(scaled).astype(jnp.bfloat16)


def pad_rows(frames):
    return padded(frames, (("rows", 2),), 1)


def conv_block(frames, kernel):
    result = lax.conv_general_dilated(
        frames[None],
        kernel,
        (1, 1, 1),
        ((0, 0), (0, 0), (1, 1)),
        dimension_numbers=("NCDHW", "DHWIO", "NCDHW"),
        preferred_element_type=jnp.float32,
    )
    return result[0]


def gathered_conv(frames, kernel):
    initial = jnp.zeros(
        (kernel.shape[4], frames.shape[1] - 2, frames.shape[2] - 2, frames.shape[3]), jnp.float32
    )
    channels = lax.all_gather(frames, "chan", axis=0, tiled=True)
    section = lax.slice_in_dim(kernel, 0, channels.shape[0], axis=3)
    return initial + conv_block(channels, section)


def kernel_columns(kernel):
    return lax.all_to_all(kernel, "chan", split_axis=4, concat_axis=3, tiled=True)


def body(
    latents, cache_one, cache_two, gain_one, bias_one, weight_one, gain_two, bias_two, weight_two
):
    floats = latents.astype(jnp.float32)
    first = group_silu(floats, gain_one, bias_one)
    frames_one = pad_rows(jnp.concatenate([cache_one, first], axis=1))
    middle = gathered_conv(frames_one, weight_one).astype(jnp.bfloat16)
    second = group_silu(middle.astype(jnp.float32), gain_two, bias_two)
    frames_two = pad_rows(jnp.concatenate([cache_two, second], axis=1))
    columns = kernel_columns(weight_two)
    outcome = gathered_conv(frames_two, columns)
    result = floats + outcome
    return jnp.repeat(jnp.repeat(result, 2, axis=2), 2, axis=3)


def solution(mesh):
    return jax.shard_map(
        body,
        mesh=mesh,
        in_specs=(
            P("chan", None, "rows", None),
            P("chan", None, "rows", None),
            P("chan", None, "rows", None),
            P("chan"),
            P("chan"),
            P(None, None, None, None, "chan"),
            P("chan"),
            P("chan"),
            P(None, None, None, "chan", None),
        ),
        out_specs=P("chan", None, "rows", None),
        check_vma=False,
    )
```

profile of v0, /device:TPU:0, one launch (start us, length us, event | category | flops | bytes accessed | tf_op | source)
XLA Modules:
  0.0 272.5 jit_solution(15219196407137967923)
XLA Ops:
  6.5 1.2 convert_reduce_fusion
  7.9 0.1 reduce_sum.54
  8.0 0.1 reduce_sum.51
  8.1 15.6 %all-reduce.1 = (f32[8]{0:T(128)S(1)}, f32[8]{0:T(128)}) all-reduce(f32[8]{0:T(128)S(1)} %reduce_sum.54, f32[8]{0:T(128)S(1)} %reduce_sum.51), channel_id=1, replica_groups=mesh['rows'=8,'chan'=4] {'rows'}, use_global_device_ids=true, to_apply=%region_5.6 | all-reduce | flops 16 | bytes 128 | tf_op jit(solution)/shard_map/psum | solution.py:27
  23.7 0.7 broadcast_multiply_fusion.1
  24.7 0.9 copy.43
  25.6 1.1 fusion.38
  26.7 1.3 collective-permute-start.1
  28.0 3.0 %collective-permute-start = (bf16[128,6,1,128]{3,0,2,1:T(8,128)(2,1)S(1)}, bf16[128,6,1,128]{3,0,2,1:T(8,128)(2,1)S(1)}, u32[]{:S(2)}, u32[]{:S(2)}) collective-permute-start(bf16[128,6,1,128]{3,0,2,1:T(8,128)(2,1)S(1)} %pad_maximum_fusion.2), channel_id=1, source_target_pairs={{0,4},{4,8},{8,12},{12,16},{16,20},{20,24},{24,28},{1,5},{5,9},{9,... | collective-permute-start | bytes 589832 | tf_op jit(solution)/shard_map/ppermute | solution.py:16
  31.1 1.0 collective-permute-done
  32.1 0.9 pad_maximum_fusion
  33.0 8.1 %copy.53 = bf16[3,3,3,128,512]{3,2,1,0,4:T(4,128)(2,1)} copy(bf16[3,3,3,128,512]{4,3,2,1,0:T(8,128)(2,1)} %param.17) | data formatting | bytes 7077888 | tf_op args[8]
  41.1 5.0 %all-to-all-start = ((bf16[3,3,3,128,512]{3,2,1,0,4:T(4,128)(2,1)}), bf16[3,3,3,128,512]{3,2,1,0,4:T(4,128)(2,1)}, u32[]{:S(2)}, u32[]{:S(2)}) async-start(bf16[3,3,3,128,512]{3,2,1,0,4:T(4,128)(2,1)} %copy.53), calls=%async_computation | async-start | bytes 9437184 | tf_op jit(solution)/shard_map/all_to_all | solution.py:64
  46.2 84.4 %all-gather.3.cloned.1.call-done = bf16[512,6,3,128]{3,0,2,1:T(8,128)(2,1)} async-done(((bf16[128,6,3,128]{3,0,2,1:T(8,128)(2,1)}), bf16[512,6,3,128]{3,0,2,1:T(8,128)(2,1)}) %all-gather.3.cloned.1.call-update) | async-done | bytes 2359312 | tf_op jit(solution)/shard_map/all_gather | solution.py:58
  130.6 4.3 %copy.61 = bf16[512,6,3,1,128]{0,4,2,1,3:T(8,128)(2,1)} copy(bf16[512,6,3,1,128]{4,0,2,1,3:T(8,128)(2,1)} %bitcast.64) | data formatting | bytes 4718592
  134.9 4.1 %pad.clone = bf16[512,6,3,1,136]{0,4,2,1,3:T(8,128)(2,1)} pad(bf16[512,6,3,1,128]{0,4,2,1,3:T(8,128)(2,1)} %copy.61, bf16[]{:T(256)} %constant.17), padding=0_0x0_0x0_0x0_0x1_7 | pad | bytes 4866050 | tf_op jit(solution)/shard_map/broadcast_in_dim | solution.py:44
  139.0 5.0 %reshape.105 = bf16[512,6,3,1,8,17]{0,5,4,2,1,3:T(8,128)(2,1)} reshape(bf16[512,6,3,1,136]{0,4,2,1,3:T(8,128)(2,1)} %pad.clone) | data formatting | bytes 5013504 | tf_op jit(solution)/shard_map/conv_general_dilated | solution.py:43
  144.0 3.1 %copy.46 = bf16[512,6,3,1,8,17]{0,4,5,2,1,3:T(8,128)(2,1)S(1)} copy(bf16[512,6,3,1,8,17]{0,5,4,2,1,3:T(8,128)(2,1)} %reshape.105) | data formatting | bytes 5013504 | tf_op jit(solution)/shard_map/conv_general_dilated | solution.py:43
  147.1 4.7 %fusion.27 = (f32[128]{0:T(128)S(1)}, f32[128]{0:T(128)S(1)}, bf16[4,1,8,17,128]{4,2,3,1,0:T(8,128)(2,1)}) fusion(pred[8,17]{0,1:T(8,128)(4,1)S(1)} %copy-done.3, bf16[3,3,3,512,128]{4,3,2,1,0:T(8,128)(2,1)S(1)} %copy-done, bf16[512,6,3,1,7,2]{0,4,5,2,1,3:T(8,128)(2,1)S(1)} %slice.4, bf16[512,6,3,1,8,17]{0,4,5,2,1,3:T(8,128)(2,1)S(1)} %copy.46), kind=kOutput, calls=%fused_computation.28 | convolution fusion | flops 1934147328 | bytes 6444168 | tf_op jit(solution)/shard_map/conv_general_dilated | solution.py:43
  151.9 0.1 reduce_sum.75
  152.1 0.1 reduce_sum.72
  152.3 1.5 copy.49
  153.7 15.1 %all-reduce = (f32[8]{0:T(128)S(1)}, f32[8]{0:T(128)}) all-reduce(f32[8]{0:T(128)S(1)} %reduce_sum.75, f32[8]{0:T(128)S(1)} %reduce_sum.72), channel_id=1, replica_groups=mesh['rows'=8,'chan'=4] {'rows'}, use_global_device_ids=true, to_apply=%region_11.12 | all-reduce | flops 16 | bytes 128 | tf_op jit(solution)/shard_map/psum | solution.py:27
  168.8 1.0 copy.47
  169.8 0.7 slice.5
  170.5 1.7 copy.59
  172.1 0.7 broadcast_multiply_fusion
  173.1 1.1 fusion.49
  174.2 0.9 pad_maximum_fusion.3
  175.1 1.3 collective-permute-start.3
  176.4 3.2 %collective-permute-start.2 = (bf16[128,6,1,128]{3,0,2,1:T(8,128)(2,1)S(1)}, bf16[128,6,1,128]{3,0,2,1:T(8,128)(2,1)S(1)}, u32[]{:S(2)}, u32[]{:S(2)}) collective-permute-start(bf16[128,6,1,128]{3,0,2,1:T(8,128)(2,1)S(1)} %pad_maximum_fusion.3), channel_id=1, source_target_pairs={{0,4},{4,8},{8,12},{12,16},{16,20},{20,24},{24,28},{1,5},{5,9},{9,... | collective-permute-start | bytes 589832 | tf_op jit(solution)/shard_map/ppermute | solution.py:16
  179.6 0.8 collective-permute-done.2
  180.5 1.7 pad_maximum_fusion.1
  182.2 5.5 %all-to-all-done = bf16[3,3,3,128,512]{3,2,1,0,4:T(4,128)(2,1)} async-done(((bf16[3,3,3,128,512]{3,2,1,0,4:T(4,128)(2,1)}), bf16[3,3,3,128,512]{3,2,1,0,4:T(4,128)(2,1)}, u32[]{:S(2)}, u32[]{:S(2)}) %all-to-all-start) | async-done | bytes 3538976 | tf_op jit(solution)/shard_map/all_to_all | solution.py:64
  187.7 8.1 %copy.54 = bf16[3,3,3,128,4,128]{5,3,4,2,1,0:T(8,128)(2,1)} copy(bf16[3,3,3,128,4,128]{3,2,1,0,5,4:T(4,128)(2,1)} %bitcast.7) | data formatting | bytes 7077888 | tf_op jit(solution)/shard_map/all_to_all | solution.py:64
  195.7 36.8 %all-gather.5.cloned.1.call-done = bf16[512,6,3,128]{3,0,2,1:T(8,128)(2,1)} async-done(((bf16[128,6,3,128]{3,0,2,1:T(8,128)(2,1)}), bf16[512,6,3,128]{3,0,2,1:T(8,128)(2,1)}) %all-gather.5.cloned.1.call-update) | async-done | bytes 2359312 | tf_op jit(solution)/shard_map/all_gather | solution.py:58
  232.5 4.3 %copy.62 = bf16[512,6,3,1,128]{0,4,2,1,3:T(8,128)(2,1)} copy(bf16[512,6,3,1,128]{4,0,2,1,3:T(8,128)(2,1)} %bitcast.65) | data formatting | bytes 4718592
  236.8 4.1 %pad.2.clone = bf16[512,6,3,1,136]{0,4,2,1,3:T(8,128)(2,1)} pad(bf16[512,6,3,1,128]{0,4,2,1,3:T(8,128)(2,1)} %copy.62, bf16[]{:T(256)} %constant.17), padding=0_0x0_0x0_0x0_0x1_7 | pad | bytes 4866050 | tf_op jit(solution)/shard_map/broadcast_in_dim | solution.py:44
  240.9 5.0 %reshape.114 = bf16[512,6,3,1,8,17]{0,5,4,2,1,3:T(8,128)(2,1)} reshape(bf16[512,6,3,1,136]{0,4,2,1,3:T(8,128)(2,1)} %pad.2.clone) | data formatting | bytes 5013504 | tf_op jit(solution)/shard_map/conv_general_dilated | solution.py:43
  245.9 3.2 %copy.52 = bf16[512,6,3,1,8,17]{0,4,5,2,1,3:T(8,128)(2,1)S(1)} copy(bf16[512,6,3,1,8,17]{0,5,4,2,1,3:T(8,128)(2,1)} %reshape.114) | data formatting | bytes 5013504 | tf_op jit(solution)/shard_map/conv_general_dilated | solution.py:43
  249.2 4.0 %fusion.18 = f32[4,1,8,17,128]{4,2,3,1,0:T(8,128)S(1)} fusion(bf16[3,3,3,512,128]{4,3,2,1,0:T(8,128)(2,1)S(1)} %bitcast.63, bf16[512,6,3,1,7,2]{0,4,5,2,1,3:T(8,128)(2,1)S(1)} %slice.6, bf16[512,6,3,1,8,17]{0,4,5,2,1,3:T(8,128)(2,1)S(1)} %copy.52, pred[8,17]{0,1:T(8,128)(4,1)S(1)} %copy-done.4), kind=kOutput, calls=%fused_computation.17 | convolution fusion | flops 1933660160 | bytes 6582408 | tf_op jit(solution)/shard_map/conv_general_dilated | solution.py:43
  253.3 0.7 slice.7
  254.1 1.8 copy.60
  255.8 1.7 fusion.40
  257.5 1.8 copy.57
  259.3 1.9 broadcast_in_dim.24
  261.2 2.0 copy.58
  263.3 2.4 broadcast_in_dim.26
  (32 shorter events, 1.3 us)
Async XLA Ops:
  6.5 140.6 %copy-start = (bf16[3,3,3,512,128]{4,3,2,1,0:T(8,128)(2,1)S(1)}, bf16[3,3,3,512,128]{4,3,2,1,0:T(8,128)(2,1)}, u32[]{:S(2)}) copy-start(bf16[3,3,3,512,128]{4,3,2,1,0:T(8,128)(2,1)} %param.14) | copy-start | bytes 10616836
  6.5 124.1 %all-gather.3.cloned.1.call-start = ((), (), s32[]{:S(2)}) async-start(), calls=%async_computation.1 | async-start | bytes 2949120 | tf_op jit(solution)/shard_map/all_gather | solution.py:58
  26.7 4.4 %collective-permute-start.1 = (bf16[128,6,1,128]{3,0,2,1:T(8,128)(2,1)S(1)}, bf16[128,6,1,128]{3,0,2,1:T(8,128)(2,1)S(1)}, u32[]{:S(2)}, u32[]{:S(2)}) collective-permute-start(bf16[128,6,1,128]{3,0,2,1:T(8,128)(2,1)S(1)} %pad_maximum_fusion.2), channel_id=1, source_target_pairs={{4,0},{8,4},{12,8},{16,12},{20,16},{24,20},{28,24},{5,1},{9,5},{13... | collective-permute-start | bytes 589832 | tf_op jit(solution)/shard_map/ppermute | solution.py:19
  28.0 4.1 %collective-permute-start = (bf16[128,6,1,128]{3,0,2,1:T(8,128)(2,1)S(1)}, bf16[128,6,1,128]{3,0,2,1:T(8,128)(2,1)S(1)}, u32[]{:S(2)}, u32[]{:S(2)}) collective-permute-start(bf16[128,6,1,128]{3,0,2,1:T(8,128)(2,1)S(1)} %pad_maximum_fusion.2), channel_id=1, source_target_pairs={{0,4},{4,8},{8,12},{12,16},{16,20},{20,24},{24,28},{1,5},{5,9},{9,... | collective-permute-start | bytes 589832 | tf_op jit(solution)/shard_map/ppermute | solution.py:16
  41.1 146.5 %all-to-all-start = ((bf16[3,3,3,128,512]{3,2,1,0,4:T(4,128)(2,1)}), bf16[3,3,3,128,512]{3,2,1,0,4:T(4,128)(2,1)}, u32[]{:S(2)}, u32[]{:S(2)}) async-start(bf16[3,3,3,128,512]{3,2,1,0,4:T(4,128)(2,1)} %copy.53), calls=%async_computation | async-start | bytes 9437184 | tf_op jit(solution)/shard_map/all_to_all | solution.py:64
  46.1 186.4 %all-gather.5.cloned.1.call-start = ((), (), s32[]{:S(2)}) async-start(), calls=%async_computation.2 | async-start | bytes 2949120 | tf_op jit(solution)/shard_map/all_gather | solution.py:58
  144.0 3.2 %copy-start.3 = (pred[8,17]{0,1:T(8,128)(4,1)S(1)}, pred[8,17]{0,1:T(8,128)(4,1)}, u32[]{:S(2)}) copy-start(pred[8,17]{0,1:T(8,128)(4,1)} %constant.27) | copy-start | bytes 412
  147.1 26.0 %copy-start.2 = (f32[128]{0:T(128)S(1)}, f32[128]{0:T(128)}, u32[]{:S(2)}) copy-start(f32[128]{0:T(128)} %param.16) | copy-start | bytes 1540
  175.1 4.5 %collective-permute-start.3 = (bf16[128,6,1,128]{3,0,2,1:T(8,128)(2,1)S(1)}, bf16[128,6,1,128]{3,0,2,1:T(8,128)(2,1)S(1)}, u32[]{:S(2)}, u32[]{:S(2)}) collective-permute-start(bf16[128,6,1,128]{3,0,2,1:T(8,128)(2,1)S(1)} %pad_maximum_fusion.3), channel_id=1, source_target_pairs={{4,0},{8,4},{12,8},{16,12},{20,16},{24,20},{28,24},{5,1},{9,5},{13... | collective-permute-start | bytes 589832 | tf_op jit(solution)/shard_map/ppermute | solution.py:19
  176.4 4.1 %collective-permute-start.2 = (bf16[128,6,1,128]{3,0,2,1:T(8,128)(2,1)S(1)}, bf16[128,6,1,128]{3,0,2,1:T(8,128)(2,1)S(1)}, u32[]{:S(2)}, u32[]{:S(2)}) collective-permute-start(bf16[128,6,1,128]{3,0,2,1:T(8,128)(2,1)S(1)} %pad_maximum_fusion.3), channel_id=1, source_target_pairs={{0,4},{4,8},{8,12},{12,16},{16,20},{20,24},{24,28},{1,5},{5,9},{9,... | collective-permute-start | bytes 589832 | tf_op jit(solution)/shard_map/ppermute | solution.py:16
  245.9 3.3 %copy-start.1 = (bf16[3,3,3,128,4,128]{5,3,4,2,1,0:T(8,128)(2,1)S(1)}, bf16[3,3,3,128,4,128]{5,3,4,2,1,0:T(8,128)(2,1)}, u32[]{:S(2)}) copy-start(bf16[3,3,3,128,4,128]{5,3,4,2,1,0:T(8,128)(2,1)} %copy.54) | copy-start | bytes 10616836
  245.9 3.3 %copy-start.4 = (pred[8,17]{0,1:T(8,128)(4,1)S(1)}, pred[8,17]{0,1:T(8,128)(4,1)}, u32[]{:S(2)}) copy-start(pred[8,17]{0,1:T(8,128)(4,1)} %constant.27) | copy-start | bytes 412
Sparse Core Ops, SparseCore 0:
  33.1 97.4 all-gather.2
  182.3 50.1 all-gather.4
where the time goes:
time: 274 us; the launch traced here: 272 us
  waiting for transfers between devices  129 us (47%)
  local copies, waits for them, and re-layouts  66.6 us (24%)
  blocking collectives  30.7 us (11%)
  starting transfers between devices  13.9 us (5%)
  between operations  13.6 us (5%)
  other arithmetic  10.4 us (4%)
  matrix products  8.76 us (3%)
    all_gather x2, waiting for transfers between devices, gathered_conv(): channels = lax.all_gather(frames, 'chan', axis=0, tiled=True)  121 us
    psum x2, blocking collectives, group_silu(): lax.psum((jnp.sum(grouped, axis=1), jnp.sum(grouped * grouped, axis=1)),...  30.7 us
    unnamed x17, local copies, waits for them, and re-layouts  22.4 us
    conv_general_dilated x8, local copies, waits for them, and re-layouts, conv_block(): lax.conv_general_dilated(frames[None], kernel, (1, 1, 1), ((0, 0), (0, 0)...  17.2 us
    conv_general_dilated x2, matrix products, conv_block(): lax.conv_general_dilated(frames[None], kernel, (1, 1, 1), ((0, 0), (0, 0)...  8.76 us
    broadcast_in_dim x2, local copies, waits for them, and re-layouts, conv_block(): frames[None]  8.19 us
    all_to_all x1, local copies, waits for them, and re-layouts, kernel_columns(): lax.all_to_all(kernel, 'chan', split_axis=4, concat_axis=3, tiled=True)  8.07 us
    broadcast_in_dim x3, local copies, waits for them, and re-layouts, body(): return jnp.repeat(jnp.repeat(result, 2, axis=2), 2, axis=3)  6.32 us
  transfers between devices with their start and end apart: 7, of which 5 were waited for; matrix products, arithmetic and copies ran while one was open for 17% of the time, Pallas kernels for 0%

commit v1 on v0

--- a/solution.py
+++ b/solution.py
@@ -6,6 +6,12 @@
 CHANNELS = 512
 GROUPS = 32
 epsilon = 1e-06
+fill_spot = lambda sample: jnp.concatenate(
+    jax.lax.all_to_all(
+        jnp.stack(jnp.split(sample, jax.lax.axis_size("chan"), axis=4)), "chan", 0, 0
+    ),
+    axis=3,
+)
 
 
 def padded(block, sides, width):
@@ -61,7 +67,7 @@
 
 
 def kernel_columns(kernel):
-    return lax.all_to_all(kernel, "chan", split_axis=4, concat_axis=3, tiled=True)
+    return fill_spot(kernel)
 
 
 def body(

time: 274 us -> 288 us (1.051)
  waiting for transfers between devices: 129 us -> 153 us
  local copies, waits for them, and re-layouts: 66.6 us -> 57.1 us
    all_gather x2, waiting for transfers between devices: 121 us -> 151 us  [gathered_conv(): channels = lax.all_gather(frames, 'chan', axis=0, tiled=True)]
    unnamed x17 -> x16, local copies, waits for them, and re-layouts: 22.4 us -> 14.4 us
    all_to_all x1 -> x0, local copies, waits for them, and re-layouts: 8.07 us -> none  [kernel_columns(): lax.all_to_all(kernel, 'chan', split_axis=4, concat_axis=3, tiled=True)]
    all_to_all x1, waiting for transfers between devices: 5.46 us -> 0.01 us  [jax.lax.all_to_all(jnp.stack(jnp.split(sample, jax.lax.axis_size('chan'),...]
    reshape x0 -> x1, local copies, waits for them, and re-layouts: none -> 4.29 us  [jnp.concatenate(jax.lax.all_to_all(jnp.stack(jnp.split(sample, jax.lax.ax...]
  transfers between devices with their start and end apart: 7 -> 7, of which waited for: 5 -> 4; matrix products, arithmetic and copies ran while one was open for 17% -> 14% of each run, Pallas kernels for 0% -> 0%
where the time goes in v1:
time: 288 us; the launch traced here: 287 us
  waiting for transfers between devices  153 us (53%)
  local copies, waits for them, and re-layouts  57.1 us (20%)
  blocking collectives  28 us (10%)
  starting transfers between devices  13.7 us (5%)
  between operations  13.6 us (5%)
  other arithmetic  12.5 us (4%)
  matrix products  8.75 us (3%)
    all_gather x2, waiting for transfers between devices, gathered_conv(): channels = lax.all_gather(frames, 'chan', axis=0, tiled=True)  151 us
    psum x2, blocking collectives, group_silu(): lax.psum((jnp.sum(grouped, axis=1), jnp.sum(grouped * grouped, axis=1)),...  28 us
    conv_general_dilated x8, local copies, waits for them, and re-layouts, conv_block(): lax.conv_general_dilated(frames[None], kernel, (1, 1, 1), ((0, 0), (0, 0)...  17.2 us
    unnamed x16, local copies, waits for them, and re-layouts  14.4 us
    conv_general_dilated x2, matrix products, conv_block(): lax.conv_general_dilated(frames[None], kernel, (1, 1, 1), ((0, 0), (0, 0)...  8.75 us
    broadcast_in_dim x2, local copies, waits for them, and re-layouts, conv_block(): frames[None]  8.28 us
    broadcast_in_dim x3, local copies, waits for them, and re-layouts, body(): return jnp.repeat(jnp.repeat(result, 2, axis=2), 2, axis=3)  6.32 us
    ppermute x2, starting transfers between devices, padded(): lax.ppermute(lax.slice_in_dim(block, block.shape[dim] - width, None, axis...  6.26 us
  transfers between devices with their start and end apart: 7, of which 4 were waited for; matrix products, arithmetic and copies ran while one was open for 14% of the time, Pallas kernels for 0%

profile of v1, /device:TPU:0, one launch (start us, length us, event | category | flops | bytes accessed | tf_op | source)
XLA Modules:
  0.0 286.9 jit_solution(17765885703045261577)
XLA Ops:
  6.5 1.2 convert_reduce_fusion
  7.9 0.1 reduce_sum.54
  8.0 0.1 reduce_sum.51
  8.1 15.6 %all-reduce.1 = (f32[8]{0:T(128)S(1)}, f32[8]{0:T(128)}) all-reduce(f32[8]{0:T(128)S(1)} %reduce_sum.54, f32[8]{0:T(128)S(1)} %reduce_sum.51), channel_id=1, replica_groups=mesh['rows'=8,'chan'=4] {'rows'}, use_global_device_ids=true, to_apply=%region_5.6 | all-reduce | flops 16 | bytes 128 | tf_op jit(solution)/shard_map/psum | solution.py:33
  23.7 0.7 broadcast_multiply_fusion.1
  24.7 0.9 copy.27
  25.6 1.1 fusion.38
  26.7 1.3 collective-permute-start.1
  28.0 3.0 %collective-permute-start = (bf16[128,6,1,128]{3,0,2,1:T(8,128)(2,1)S(1)}, bf16[128,6,1,128]{3,0,2,1:T(8,128)(2,1)S(1)}, u32[]{:S(2)}, u32[]{:S(2)}) collective-permute-start(bf16[128,6,1,128]{3,0,2,1:T(8,128)(2,1)S(1)} %pad_maximum_fusion.3), channel_id=1, source_target_pairs={{0,4},{4,8},{8,12},{12,16},{16,20},{20,24},{24,28},{1,5},{5,9},{9,... | collective-permute-start | bytes 589832 | tf_op jit(solution)/shard_map/ppermute | solution.py:22
  31.1 1.0 collective-permute-done
  32.1 0.9 pad_maximum_fusion.1
  33.0 2.3 slice_bitcast_fusion.3
  35.3 2.1 pad_maximum_fusion
  37.4 4.9 %all-to-all-start = ((bf16[4,3,3,3,128,128]{5,4,3,2,1,0:T(8,128)(2,1)}), bf16[4,3,3,3,128,128]{5,4,3,2,1,0:T(8,128)(2,1)}, u32[]{:S(2)}, u32[]{:S(2)}) async-start(bf16[4,3,3,3,128,128]{5,4,3,2,1,0:T(8,128)(2,1)} %pad_maximum_fusion), calls=%async_computation | async-start | bytes 7077888 | tf_op jit(solution)/shard_map/all_to_all | solution.py:10
  42.2 100.9 %all-gather.3.cloned.1.call-done = bf16[512,6,3,128]{3,0,2,1:T(8,128)(2,1)} async-done(((bf16[128,6,3,128]{3,0,2,1:T(8,128)(2,1)}), bf16[512,6,3,128]{3,0,2,1:T(8,128)(2,1)}) %all-gather.3.cloned.1.call-update) | async-done | bytes 2359312 | tf_op jit(solution)/shard_map/all_gather | solution.py:64
  143.2 4.3 %copy.44 = bf16[512,6,3,1,128]{0,4,2,1,3:T(8,128)(2,1)} copy(bf16[512,6,3,1,128]{4,0,2,1,3:T(8,128)(2,1)} %bitcast.70) | data formatting | bytes 4718592
  147.4 4.2 %pad.clone = bf16[512,6,3,1,136]{0,4,2,1,3:T(8,128)(2,1)} pad(bf16[512,6,3,1,128]{0,4,2,1,3:T(8,128)(2,1)} %copy.44, bf16[]{:T(256)} %constant.17), padding=0_0x0_0x0_0x0_0x1_7 | pad | bytes 4866050 | tf_op jit(solution)/shard_map/broadcast_in_dim | solution.py:50
  151.6 5.0 %reshape.113 = bf16[512,6,3,1,8,17]{0,5,4,2,1,3:T(8,128)(2,1)} reshape(bf16[512,6,3,1,136]{0,4,2,1,3:T(8,128)(2,1)} %pad.clone) | data formatting | bytes 5013504 | tf_op jit(solution)/shard_map/conv_general_dilated | solution.py:49
  156.7 3.1 %copy.30 = bf16[512,6,3,1,8,17]{0,4,5,2,1,3:T(8,128)(2,1)S(1)} copy(bf16[512,6,3,1,8,17]{0,5,4,2,1,3:T(8,128)(2,1)} %reshape.113) | data formatting | bytes 5013504 | tf_op jit(solution)/shard_map/conv_general_dilated | solution.py:49
  159.8 4.7 %fusion.27 = (f32[128]{0:T(128)S(1)}, f32[128]{0:T(128)S(1)}, bf16[4,1,8,17,128]{4,2,3,1,0:T(8,128)(2,1)}) fusion(pred[8,17]{0,1:T(8,128)(4,1)S(1)} %copy-done.3, bf16[3,3,3,512,128]{4,3,2,1,0:T(8,128)(2,1)S(1)} %copy-done, bf16[512,6,3,1,7,2]{0,4,5,2,1,3:T(8,128)(2,1)S(1)} %slice.4, bf16[512,6,3,1,8,17]{0,4,5,2,1,3:T(8,128)(2,1)S(1)} %copy.30), kind=kOutput, calls=%fused_computation.33 | convolution fusion | flops 1934147328 | bytes 6444168 | tf_op jit(solution)/shard_map/conv_general_dilated | solution.py:49
  164.6 0.1 reduce_sum.75
  164.8 0.1 reduce_sum.72
  164.9 1.5 copy.33
  166.4 12.4 %all-reduce = (f32[8]{0:T(128)S(1)}, f32[8]{0:T(128)}) all-reduce(f32[8]{0:T(128)S(1)} %reduce_sum.75, f32[8]{0:T(128)S(1)} %reduce_sum.72), channel_id=1, replica_groups=mesh['rows'=8,'chan'=4] {'rows'}, use_global_device_ids=true, to_apply=%region_11.12 | all-reduce | flops 16 | bytes 128 | tf_op jit(solution)/shard_map/psum | solution.py:33
  178.8 1.0 copy.31
  179.8 0.7 slice.5
  180.5 1.7 copy.42
  182.2 0.7 broadcast_multiply_fusion
  183.1 1.1 fusion.49
  184.2 0.9 pad_maximum_fusion.4
  185.1 1.3 collective-permute-start.3
  186.4 3.2 %collective-permute-start.2 = (bf16[128,6,1,128]{3,0,2,1:T(8,128)(2,1)S(1)}, bf16[128,6,1,128]{3,0,2,1:T(8,128)(2,1)S(1)}, u32[]{:S(2)}, u32[]{:S(2)}) collective-permute-start(bf16[128,6,1,128]{3,0,2,1:T(8,128)(2,1)S(1)} %pad_maximum_fusion.4), channel_id=1, source_target_pairs={{0,4},{4,8},{8,12},{12,16},{16,20},{20,24},{24,28},{1,5},{5,9},{9,... | collective-permute-start | bytes 589832 | tf_op jit(solution)/shard_map/ppermute | solution.py:22
  189.6 0.8 collective-permute-done.2
  190.5 1.7 pad_maximum_fusion.2
  192.2 4.3 %copy.37 = bf16[3,3,3,4,128,128]{5,4,3,2,1,0:T(8,128)(2,1)} copy(bf16[3,3,3,4,128,128]{5,4,2,1,0,3:T(8,128)(2,1)} %bitcast.11) | data formatting | bytes 7077888 | tf_op jit(solution)/shard_map/reshape | solution.py:9
  196.5 50.4 %all-gather.5.cloned.1.call-done = bf16[512,6,3,128]{3,0,2,1:T(8,128)(2,1)} async-done(((bf16[128,6,3,128]{3,0,2,1:T(8,128)(2,1)}), bf16[512,6,3,128]{3,0,2,1:T(8,128)(2,1)}) %all-gather.5.cloned.1.call-update) | async-done | bytes 2359312 | tf_op jit(solution)/shard_map/all_gather | solution.py:64
  246.9 4.3 %copy.45 = bf16[512,6,3,1,128]{0,4,2,1,3:T(8,128)(2,1)} copy(bf16[512,6,3,1,128]{4,0,2,1,3:T(8,128)(2,1)} %bitcast.71) | data formatting | bytes 4718592
  251.2 4.1 %pad.2.clone = bf16[512,6,3,1,136]{0,4,2,1,3:T(8,128)(2,1)} pad(bf16[512,6,3,1,128]{0,4,2,1,3:T(8,128)(2,1)} %copy.45, bf16[]{:T(256)} %constant.17), padding=0_0x0_0x0_0x0_0x1_7 | pad | bytes 4866050 | tf_op jit(solution)/shard_map/broadcast_in_dim | solution.py:50
  255.3 5.0 %reshape.122 = bf16[512,6,3,1,8,17]{0,5,4,2,1,3:T(8,128)(2,1)} reshape(bf16[512,6,3,1,136]{0,4,2,1,3:T(8,128)(2,1)} %pad.2.clone) | data formatting | bytes 5013504 | tf_op jit(solution)/shard_map/conv_general_dilated | solution.py:49
  260.3 3.2 %copy.36 = bf16[512,6,3,1,8,17]{0,4,5,2,1,3:T(8,128)(2,1)S(1)} copy(bf16[512,6,3,1,8,17]{0,5,4,2,1,3:T(8,128)(2,1)} %reshape.122) | data formatting | bytes 5013504 | tf_op jit(solution)/shard_map/conv_general_dilated | solution.py:49
  263.6 4.0 %fusion.18 = f32[4,1,8,17,128]{4,2,3,1,0:T(8,128)S(1)} fusion(bf16[3,3,3,512,128]{4,3,2,1,0:T(8,128)(2,1)S(1)} %bitcast.69, bf16[512,6,3,1,7,2]{0,4,5,2,1,3:T(8,128)(2,1)S(1)} %slice.6, bf16[512,6,3,1,8,17]{0,4,5,2,1,3:T(8,128)(2,1)S(1)} %copy.36, pred[8,17]{0,1:T(8,128)(4,1)S(1)} %copy-done.4), kind=kOutput, calls=%fused_computation.18 | convolution fusion | flops 1933660160 | bytes 6582408 | tf_op jit(solution)/shard_map/conv_general_dilated | solution.py:49
  267.7 0.7 slice.7
  268.5 1.8 copy.43
  270.2 1.7 fusion.40
  271.9 1.8 copy.40
  273.7 1.9 broadcast_in_dim.24
  275.6 2.0 copy.41
  277.7 2.4 broadcast_in_dim.26
  (33 shorter events, 1.2 us)
Async XLA Ops:
  6.5 153.3 %copy-start = (bf16[3,3,3,512,128]{4,3,2,1,0:T(8,128)(2,1)S(1)}, bf16[3,3,3,512,128]{4,3,2,1,0:T(8,128)(2,1)}, u32[]{:S(2)}) copy-start(bf16[3,3,3,512,128]{4,3,2,1,0:T(8,128)(2,1)} %param.14) | copy-start | bytes 10616836
  6.5 136.6 %all-gather.3.cloned.1.call-start = ((), (), s32[]{:S(2)}) async-start(), calls=%async_computation.1 | async-start | bytes 2949120 | tf_op jit(solution)/shard_map/all_gather | solution.py:64
  26.7 4.4 %collective-permute-start.1 = (bf16[128,6,1,128]{3,0,2,1:T(8,128)(2,1)S(1)}, bf16[128,6,1,128]{3,0,2,1:T(8,128)(2,1)S(1)}, u32[]{:S(2)}, u32[]{:S(2)}) collective-permute-start(bf16[128,6,1,128]{3,0,2,1:T(8,128)(2,1)S(1)} %pad_maximum_fusion.3), channel_id=1, source_target_pairs={{4,0},{8,4},{12,8},{16,12},{20,16},{24,20},{28,24},{5,1},{9,5},{13... | collective-permute-start | bytes 589832 | tf_op jit(solution)/shard_map/ppermute | solution.py:25
  28.0 4.1 %collective-permute-start = (bf16[128,6,1,128]{3,0,2,1:T(8,128)(2,1)S(1)}, bf16[128,6,1,128]{3,0,2,1:T(8,128)(2,1)S(1)}, u32[]{:S(2)}, u32[]{:S(2)}) collective-permute-start(bf16[128,6,1,128]{3,0,2,1:T(8,128)(2,1)S(1)} %pad_maximum_fusion.3), channel_id=1, source_target_pairs={{0,4},{4,8},{8,12},{12,16},{16,20},{20,24},{24,28},{1,5},{5,9},{9,... | collective-permute-start | bytes 589832 | tf_op jit(solution)/shard_map/ppermute | solution.py:22
  37.4 154.9 %all-to-all-start = ((bf16[4,3,3,3,128,128]{5,4,3,2,1,0:T(8,128)(2,1)}), bf16[4,3,3,3,128,128]{5,4,3,2,1,0:T(8,128)(2,1)}, u32[]{:S(2)}, u32[]{:S(2)}) async-start(bf16[4,3,3,3,128,128]{5,4,3,2,1,0:T(8,128)(2,1)} %pad_maximum_fusion), calls=%async_computation | async-start | bytes 7077888 | tf_op jit(solution)/shard_map/all_to_all | solution.py:10
  42.2 204.7 %all-gather.5.cloned.1.call-start = ((), (), s32[]{:S(2)}) async-start(), calls=%async_computation.2 | async-start | bytes 2949120 | tf_op jit(solution)/shard_map/all_gather | solution.py:64
  156.7 3.2 %copy-start.3 = (pred[8,17]{0,1:T(8,128)(4,1)S(1)}, pred[8,17]{0,1:T(8,128)(4,1)}, u32[]{:S(2)}) copy-start(pred[8,17]{0,1:T(8,128)(4,1)} %constant.27) | copy-start | bytes 412
  159.8 23.3 %copy-start.2 = (f32[128]{0:T(128)S(1)}, f32[128]{0:T(128)}, u32[]{:S(2)}) copy-start(f32[128]{0:T(128)} %param.16) | copy-start | bytes 1540
  185.1 4.5 %collective-permute-start.3 = (bf16[128,6,1,128]{3,0,2,1:T(8,128)(2,1)S(1)}, bf16[128,6,1,128]{3,0,2,1:T(8,128)(2,1)S(1)}, u32[]{:S(2)}, u32[]{:S(2)}) collective-permute-start(bf16[128,6,1,128]{3,0,2,1:T(8,128)(2,1)S(1)} %pad_maximum_fusion.4), channel_id=1, source_target_pairs={{4,0},{8,4},{12,8},{16,12},{20,16},{24,20},{28,24},{5,1},{9,5},{13... | collective-permute-start | bytes 589832 | tf_op jit(solution)/shard_map/ppermute | solution.py:25
  186.4 4.1 %collective-permute-start.2 = (bf16[128,6,1,128]{3,0,2,1:T(8,128)(2,1)S(1)}, bf16[128,6,1,128]{3,0,2,1:T(8,128)(2,1)S(1)}, u32[]{:S(2)}, u32[]{:S(2)}) collective-permute-start(bf16[128,6,1,128]{3,0,2,1:T(8,128)(2,1)S(1)} %pad_maximum_fusion.4), channel_id=1, source_target_pairs={{0,4},{4,8},{8,12},{12,16},{16,20},{20,24},{24,28},{1,5},{5,9},{9,... | collective-permute-start | bytes 589832 | tf_op jit(solution)/shard_map/ppermute | solution.py:22
  260.3 3.3 %copy-start.1 = (bf16[3,3,3,4,128,128]{5,4,3,2,1,0:T(8,128)(2,1)S(1)}, bf16[3,3,3,4,128,128]{5,4,3,2,1,0:T(8,128)(2,1)}, u32[]{:S(2)}) copy-start(bf16[3,3,3,4,128,128]{5,4,3,2,1,0:T(8,128)(2,1)} %copy.37) | copy-start | bytes 10616836
  260.3 3.3 %copy-start.4 = (pred[8,17]{0,1:T(8,128)(4,1)S(1)}, pred[8,17]{0,1:T(8,128)(4,1)}, u32[]{:S(2)}) copy-start(pred[8,17]{0,1:T(8,128)(4,1)} %constant.27) | copy-start | bytes 412
Sparse Core Ops, SparseCore 0:
  33.1 109.9 all-gather.2
  192.4 54.4 all-gather.4
